TPU v7x, 256 devices: a whole 4x4x8 slice. The times are simulated.
256 devices in a mesh: term: 32 (over z_hi, x, core), sector: 8 (over y, z_lo).
Axes of the slice: x: 4, y: 4, z: 8 (z_hi: 4, z_lo: 2; z = z_hi * 2 + z_lo), core: 2. Of those that a mesh axis runs over, the one named last changes fastest.
Arguments:
- wave: float32 [8, 512, 512], P('sector', 'term'), may hold values from -6 to 6
- left_ops: bfloat16 [256, 8, 512, 512], P('term', 'sector'), may hold values from -1 to 1
- right_ops: bfloat16 [256, 8, 512, 512], P('term', 'sector'), may hold values from -4 to 1
- diagonal: float32 [8, 512, 512], P('sector', 'term'), may hold values from -21 to 0
- block_size: int32 [8], replicated, may hold values from 128 to 512, as said below
- source: int32 [256, 8], P('term'), may hold values from 0 to 7, as said below
Outputs:
- new_vector: float32 [8, 512, 512], P('sector', 'term')
- new_sigma: float32 [8, 512, 512], P('sector', 'term')
- subspace: float32 [2, 2], replicated
Inputs may be any that keep to these rules, and one draw needn't show every extreme that they name: `block_size`: every block size lies between 128 and 512; some sector has exactly 512. `source`: entries name sectors.
All inputs are finite; a program needn't handle non-finite values.
Results may differ from a plain program's by a relative error of at most 0.005.
Values may be sent and summed in bfloat16 or wider, within the bound.
A program may use at most 64 MiB of HBM per device.

v0:
```python
import jax
import jax.numpy as jnp
from jax import lax
from jax.sharding import PartitionSpec as P


def local(wave, left_ops, right_ops, diagonal, block_size, source):
    sec_dev = wave.shape[0]
    slab_rows = wave.shape[1]
    width = wave.shape[2]
    total = float(block_size.shape[0] * width * width)
    first_row = lax.axis_index("term") * slab_rows
    first_sector = lax.axis_index("sector") * sec_dev
    sizes_owned = lax.dynamic_slice_in_dim(block_size, first_sector, sec_dev)
    row_index = first_row + jnp.arange(slab_rows)
    col_index = jnp.arange(width)
    valid = (
        (row_index[None, :, None] < sizes_owned[:, None, None])
        & (col_index[None, None, :] < sizes_owned[:, None, None])
    ).astype(jnp.float32)
    sources = lax.dynamic_slice_in_dim(source, first_sector, sec_dev, 1)
    masked = wave * valid
    squares = lax.psum(jnp.sum(masked * masked), ("term", "sector"))
    first_vec = masked / jnp.sqrt(squares / total + 1e-06)

    def apply_ham(vector):
        vector_b = vector.astype(jnp.bfloat16)
        blocks = lax.all_gather(vector_b, "term", axis=1, tiled=True)
        every_block = lax.all_gather(blocks, "sector", axis=0, tiled=True)
        chosen = jnp.take(every_block, sources, axis=0)
        halfway = jnp.einsum(
            "tpij,tpjk->tpik", left_ops, chosen, preferred_element_type=jnp.float32
        )
        halfway_b = halfway.astype(jnp.bfloat16)
        partial_sum = jnp.einsum(
            "tpij,tpkj->pik", halfway_b, right_ops, preferred_element_type=jnp.float32
        )
        owned = lax.psum_scatter(partial_sum, "term", scatter_dimension=1, tiled=True)
        return owned * valid

    first_sigma = apply_ham(first_vec)
    theta = lax.psum(jnp.sum(first_vec * first_sigma), ("term", "sector")) / total
    correction = (first_sigma - theta * first_vec) / jnp.maximum(jnp.abs(diagonal - theta), 1.0)
    correlation = lax.psum(jnp.sum(first_vec * correction), ("term", "sector")) / total
    orth = correction - correlation * first_vec
    orth_sq = lax.psum(jnp.sum(orth * orth), ("term", "sector")) / total
    new_vector = orth / jnp.sqrt(orth_sq + 1e-06)
    new_sigma = apply_ham(new_vector)
    upper, lower, corner = lax.psum(
        (
            jnp.sum(first_vec * new_sigma),
            jnp.sum(new_vector * first_sigma),
            jnp.sum(new_vector * new_sigma),
        ),
        ("term", "sector"),
    )
    subspace = jnp.stack(
        [jnp.stack([theta, upper / total]), jnp.stack([lower / total, corner / total])]
    )
    return (new_vector, new_sigma, subspace)


def solution(mesh):
    return jax.shard_map(
        local,
        mesh=mesh,
        in_specs=(
            P("sector", "term", None),
            P("term", "sector", None, None),
            P("term", "sector", None, None),
            P("sector", "term", None),
            P(),
            P("term", None),
        ),
        out_specs=(P("sector", "term", None), P("sector", "term", None), P()),
        check_vma=False,
    )
```

profile of v0, /device:TPU:1, one launch (start us, length us, event | category | flops | bytes accessed | tf_op | source)
XLA Modules:
  0.0 882.0 jit_solution(14392173964076206759)
XLA Ops:
  7.2 1.2 dynamic_slice.6
  9.8 1.4 multiply_reduce_fusion.6
  11.2 81.4 %psum.49 = f32[]{:T(128)} all-reduce(f32[]{:T(128)} %multiply_reduce_fusion.6), channel_id=1, replica_groups=mesh['term'=32,'sector'=8] {'term','sector'}, use_global_device_ids=true, to_apply=%region_1.0 | all-reduce | flops 1 | bytes 8 | tf_op jit(solution)/shard_map/psum | solution.py:23
  93.3 0.8 fusion.50
  94.1 44.1 %all_gather.12 = bf16[1,512,512]{2,1,0:T(8,128)(2,1)} all-gather(bf16[1,16,512]{2,1,0:T(8,128)(2,1)S(1)} %fusion.50), channel_id=1, replica_groups=mesh['term'=32,'sector'=8] {'term'}, dimensions={1}, use_global_device_ids=true | all-gather | bytes 540672 | tf_op jit(solution)/shard_map/all_gather | solution.py:28
  138.3 0.9 fusion.45
  139.2 0.9 and_reduce_fusion
  140.1 86.3 %all-gather.3.cloned.1.call-done = bf16[8,512,512]{2,1,0:T(8,128)(2,1)} async-done(((bf16[1,512,512]{2,1,0:T(8,128)(2,1)}), bf16[8,512,512]{2,1,0:T(8,128)(2,1)}) %all-gather.3.cloned.1.call-update) | async-done | bytes 4194320 | tf_op jit(solution)/shard_map/all_gather | solution.py:29
  226.3 5.0 gather_fusion
  231.3 10.3 %fusion.18 = f32[1,512,512]{2,1,0:T(8,128)} fusion(bf16[8,1,512,512]{3,2,1,0:T(8,128)(2,1)} %param.10, bf16[8,1,512,512]{3,2,1,0:T(8,128)(2,1)} %param.9, bf16[8,512,512]{2,1,0:T(8,128)(2,1)} %gather_fusion, pred[8]{0:T(512)(128)(4,1)S(1)} %and_reduce_fusion), kind=kOutput, calls=%fused_computation.22 | convolution fusion | flops 4299161600 | bytes 13631496 | tf_op jit(solution)/shard_map/tpij,tpkj->pik/dot_general | solution.py:35
  241.7 87.8 %reduce-scatter.3.cloned.1.call-done = f32[1,16,512]{2,1,0:T(8,128)} async-done(((f32[1,512,512]{2,1,0:T(8,128)}), f32[1,16,512]{2,1,0:T(8,128)}) %reduce-scatter.3.cloned.1.call-update) | async-done | bytes 32784 | tf_op jit(solution)/shard_map/reduce_scatter | solution.py:38
  329.5 1.4 multiply_reduce_fusion.5
  330.9 75.8 %psum.50 = f32[]{:T(128)} all-reduce(f32[]{:T(128)} %multiply_reduce_fusion.5), channel_id=1, replica_groups=mesh['term'=32,'sector'=8] {'term','sector'}, use_global_device_ids=true, to_apply=%region_4.6 | all-reduce | flops 1 | bytes 8 | tf_op jit(solution)/shard_map/psum | solution.py:42
  407.3 1.5 multiply_reduce_fusion.4
  408.8 73.4 %psum.51 = f32[]{:T(128)} all-reduce(f32[]{:T(128)} %get-tuple-element.13), channel_id=1, replica_groups=mesh['term'=32,'sector'=8] {'term','sector'}, use_global_device_ids=true, to_apply=%region_6.8 | all-reduce | flops 1 | bytes 8 | tf_op jit(solution)/shard_map/psum | solution.py:44
  482.8 0.7 multiply_reduce_fusion.3
  483.5 73.4 %psum.52 = f32[]{:T(128)} all-reduce(f32[]{:T(128)} %multiply_reduce_fusion.3), channel_id=1, replica_groups=mesh['term'=32,'sector'=8] {'term','sector'}, use_global_device_ids=true, to_apply=%region_8.10 | all-reduce | flops 1 | bytes 8 | tf_op jit(solution)/shard_map/psum | solution.py:46
  557.7 46.8 %all_gather.14 = bf16[1,512,512]{2,1,0:T(8,128)(2,1)} all-gather(bf16[1,16,512]{2,1,0:T(8,128)(2,1)S(1)} %get-tuple-element.11), channel_id=1, replica_groups=mesh['term'=32,'sector'=8] {'term'}, dimensions={1}, use_global_device_ids=true | all-gather | bytes 540672 | tf_op jit(solution)/shard_map/all_gather | solution.py:28
  604.7 87.0 %all-gather.5.cloned.1.call-done = bf16[8,512,512]{2,1,0:T(8,128)(2,1)} async-done(((bf16[1,512,512]{2,1,0:T(8,128)(2,1)}), bf16[8,512,512]{2,1,0:T(8,128)(2,1)}) %all-gather.5.cloned.1.call-update) | async-done | bytes 4194320 | tf_op jit(solution)/shard_map/all_gather | solution.py:29
  691.8 5.0 gather_fusion.1
  696.7 10.3 %fusion.23 = f32[1,512,512]{2,1,0:T(8,128)} fusion(bf16[8,1,512,512]{3,2,1,0:T(8,128)(2,1)} %param.10, bf16[8,512,512]{2,1,0:T(8,128)(2,1)} %gather_fusion.1, bf16[8,1,512,512]{3,2,1,0:T(8,128)(2,1)} %param.9, pred[8]{0:T(512)(128)(4,1)S(1)} %and_reduce_fusion), kind=kOutput, calls=%fused_computation.23 | convolution fusion | flops 4299161600 | bytes 13631496 | tf_op jit(solution)/shard_map/tpij,tpkj->pik/dot_general | solution.py:35
  707.0 87.9 %reduce-scatter.5.cloned.1.call-done = f32[1,16,512]{2,1,0:T(8,128)} async-done(((f32[1,512,512]{2,1,0:T(8,128)}), f32[1,16,512]{2,1,0:T(8,128)}) %reduce-scatter.5.cloned.1.call-update) | async-done | bytes 32784 | tf_op jit(solution)/shard_map/reduce_scatter | solution.py:38
  794.9 2.1 multiply_reduce_fusion.2
  797.0 76.0 %all-reduce = (f32[]{:T(128)}, f32[]{:T(128)}, f32[]{:T(128)}) all-reduce(f32[]{:T(128)} %get-tuple-element.5, f32[]{:T(128)} %get-tuple-element.6, f32[]{:T(128)} %get-tuple-element.4), channel_id=1, replica_groups=mesh['term'=32,'sector'=8] {'term','sector'}, use_global_device_ids=true, to_apply=%region_15.17 | all-reduce | flops 3 | bytes 24 | tf_op jit(solution)/shard_map/psum | solution.py:49
  (22 shorter events, 2.5 us)
Async XLA Ops:
  7.2 219.2 %all-gather.3.cloned.1.call-start = ((), (), s32[]{:S(2)}) async-start(), calls=%async_computation.2 | async-start | bytes 4718592 | tf_op jit(solution)/shard_map/all_gather | solution.py:29
  138.2 191.2 %reduce-scatter.3.cloned.1.call-start = ((), (), s32[]{:S(2)}) async-start(), calls=%async_computation.3 | async-start | bytes 1081344 | tf_op jit(solution)/shard_map/reduce_scatter | solution.py:38
  231.3 98.2 %copy-start = (f32[1,16,512]{2,1,0:T(8,128)S(1)}, f32[1,16,512]{2,1,0:T(8,128)}, u32[]{:S(2)}) copy-start(f32[1,16,512]{2,1,0:T(8,128)} %param.8) | copy-start | bytes 98308
  231.3 176.0 %copy-start.3 = (f32[1,16,512]{2,1,0:T(8,128)S(1)}, f32[1,16,512]{2,1,0:T(8,128)}, u32[]{:S(2)}) copy-start(f32[1,16,512]{2,1,0:T(8,128)} %param.11) | copy-start | bytes 98308
  241.6 450.2 %all-gather.5.cloned.1.call-start = ((), (), s32[]{:S(2)}) async-start(), calls=%async_computation.4 | async-start | bytes 4718592 | tf_op jit(solution)/shard_map/all_gather | solution.py:29
  557.7 237.2 %copy-start.2 = (f32[1,16,512]{2,1,0:T(8,128)}, f32[1,16,512]{2,1,0:T(8,128)S(1)}, u32[]{:S(2)}) copy-start(f32[1,16,512]{2,1,0:T(8,128)S(1)} %get-tuple-element.12) | copy-start | bytes 98308
  604.5 190.4 %reduce-scatter.5.cloned.1.call-start = ((), (), s32[]{:S(2)}) async-start(), calls=%async_computation.5 | async-start | bytes 1081344 | tf_op jit(solution)/shard_map/reduce_scatter | solution.py:38
  696.7 98.2 %copy-start.1 = (f32[1,16,512]{2,1,0:T(8,128)S(1)}, f32[1,16,512]{2,1,0:T(8,128)}, u32[]{:S(2)}) copy-start(f32[1,16,512]{2,1,0:T(8,128)} %reduce-scatter.3.cloned.1.call-done) | copy-start | bytes 98308
Sparse Core Ops, SparseCore 0:
  138.4 87.9 all-gather.2
  241.7 87.6 reduce-scatter.2
  604.6 87.1 all-gather.4
  707.1 87.6 reduce-scatter.4
where the time goes:
time: 883 us; the launch traced here: 882 us
  blocking collectives  471 us (53%)
  waiting for transfers between devices  349 us (40%)
  matrix products  20.5 us (2%)
  between operations  18.4 us (2%)
  other arithmetic  11.8 us (1%)
  local copies, waits for them, and re-layouts  11.2 us (1%)
    reduce_scatter x2, waiting for transfers between devices, apply_ham(): lax.psum_scatter(partial_sum, 'term', scatter_dimension=1, tiled=True)  176 us
    all_gather x2, waiting for transfers between devices, apply_ham(): every_block = lax.all_gather(blocks, 'sector', axis=0, tiled=True)  173 us
    all_gather x2, blocking collectives, apply_ham(): blocks = lax.all_gather(vector_b, 'term', axis=1, tiled=True)  90.9 us
    psum x1, blocking collectives, local(): squares = lax.psum(jnp.sum(masked * masked), ('term', 'sector'))  81.4 us
    psum x1, blocking collectives, local(): lax.psum((jnp.sum(first_vec * new_sigma), jnp.sum(new_vector * first_sigm...  76 us
    psum x1, blocking collectives, local(): lax.psum(jnp.sum(first_vec * first_sigma), ('term', 'sector')) / total  75.8 us
    psum x1, blocking collectives, local(): orth_sq = lax.psum(jnp.sum(orth * orth), ('term', 'sector')) / total  73.4 us
    psum x1, blocking collectives, local(): lax.psum(jnp.sum(first_vec * correction), ('term', 'sector')) / total  73.4 us
  transfers between devices with their start and end apart: 4, of which 4 were waited for; matrix products, arithmetic and copies ran while one was open for 0% of the time, Pallas kernels for 0%

commit v1 on v0

--- a/solution.py
+++ b/solution.py
@@ -47,12 +47,15 @@
     new_vector = orth / jnp.sqrt(orth_sq + 1e-06)
     new_sigma = apply_ham(new_vector)
     upper, lower, corner = lax.psum(
-        (
-            jnp.sum(first_vec * new_sigma),
-            jnp.sum(new_vector * first_sigma),
-            jnp.sum(new_vector * new_sigma),
+        lax.psum(
+            (
+                jnp.sum(first_vec * new_sigma),
+                jnp.sum(new_vector * first_sigma),
+                jnp.sum(new_vector * new_sigma),
+            ),
+            "sector",
         ),
-        ("term", "sector"),
+        "term",
     )
     subspace = jnp.stack(
         [jnp.stack([theta, upper / total]), jnp.stack([lower / total, corner / total])]

time: 883 us -> 899 us (1.018)
  blocking collectives: 471 us -> 487 us
    psum x0 -> x1, blocking collectives: none -> 76.3 us  [local(): lax.psum(lax.psum((jnp.sum(first_vec * new_sigma), jnp.sum(new_vector * f...]
    psum x1, blocking collectives: 76 us -> 15.8 us  [local(): lax.psum((jnp.sum(first_vec * new_sigma), jnp.sum(new_vector * first_sigm...]
where the time goes in v1:
time: 899 us; the launch traced here: 898 us
  blocking collectives  487 us (54%)
  waiting for transfers between devices  349 us (39%)
  matrix products  20.5 us (2%)
  between operations  18.4 us (2%)
  other arithmetic  11.8 us (1%)
  local copies, waits for them, and re-layouts  11.2 us (1%)
    reduce_scatter x2, waiting for transfers between devices, apply_ham(): lax.psum_scatter(partial_sum, 'term', scatter_dimension=1, tiled=True)  176 us
    all_gather x2, waiting for transfers between devices, apply_ham(): every_block = lax.all_gather(blocks, 'sector', axis=0, tiled=True)  173 us
    all_gather x2, blocking collectives, apply_ham(): blocks = lax.all_gather(vector_b, 'term', axis=1, tiled=True)  90.9 us
    psum x1, blocking collectives, local(): squares = lax.psum(jnp.sum(masked * masked), ('term', 'sector'))  81.3 us
    psum x1, blocking collectives, local(): lax.psum(lax.psum((jnp.sum(first_vec * new_sigma), jnp.sum(new_vector * f...  76.3 us
    psum x1, blocking collectives, local(): lax.psum(jnp.sum(first_vec * first_sigma), ('term', 'sector')) / total  75.7 us
    psum x1, blocking collectives, local(): orth_sq = lax.psum(jnp.sum(orth * orth), ('term', 'sector')) / total  73.4 us
    psum x1, blocking collectives, local(): lax.psum(jnp.sum(first_vec * correction), ('term', 'sector')) / total  73.4 us
  transfers between devices with their start and end apart: 4, of which 4 were waited for; matrix products, arithmetic and copies ran while one was open for 0% of the time, Pallas kernels for 0%

profile of v1, /device:TPU:1, one launch (start us, length us, event | category | flops | bytes accessed | tf_op | source)
XLA Modules:
  0.0 898.1 jit_solution(9890674897010639413)
XLA Ops:
  7.2 1.2 dynamic_slice.6
  9.8 1.4 multiply_reduce_fusion.6
  11.2 81.3 %psum.70 = f32[]{:T(128)} all-reduce(f32[]{:T(128)} %multiply_reduce_fusion.6), channel_id=1, replica_groups=mesh['term'=32,'sector'=8] {'term','sector'}, use_global_device_ids=true, to_apply=%region_1.0 | all-reduce | flops 1 | bytes 8 | tf_op jit(solution)/shard_map/psum | solution.py:23
  93.3 0.8 fusion.50
  94.1 44.1 %all_gather.12 = bf16[1,512,512]{2,1,0:T(8,128)(2,1)} all-gather(bf16[1,16,512]{2,1,0:T(8,128)(2,1)S(1)} %fusion.50), channel_id=1, replica_groups=mesh['term'=32,'sector'=8] {'term'}, dimensions={1}, use_global_device_ids=true | all-gather | bytes 540672 | tf_op jit(solution)/shard_map/all_gather | solution.py:28
  138.3 0.9 fusion.45
  139.2 0.9 and_reduce_fusion
  140.0 86.3 %all-gather.3.cloned.1.call-done = bf16[8,512,512]{2,1,0:T(8,128)(2,1)} async-done(((bf16[1,512,512]{2,1,0:T(8,128)(2,1)}), bf16[8,512,512]{2,1,0:T(8,128)(2,1)}) %all-gather.3.cloned.1.call-update) | async-done | bytes 4194320 | tf_op jit(solution)/shard_map/all_gather | solution.py:29
  226.3 5.0 gather_fusion
  231.3 10.3 %fusion.18 = f32[1,512,512]{2,1,0:T(8,128)} fusion(bf16[8,1,512,512]{3,2,1,0:T(8,128)(2,1)} %param.10, bf16[8,1,512,512]{3,2,1,0:T(8,128)(2,1)} %param.9, bf16[8,512,512]{2,1,0:T(8,128)(2,1)} %gather_fusion, pred[8]{0:T(512)(128)(4,1)S(1)} %and_reduce_fusion), kind=kOutput, calls=%fused_computation.22 | convolution fusion | flops 4299161600 | bytes 13631496 | tf_op jit(solution)/shard_map/tpij,tpkj->pik/dot_general | solution.py:35
  241.6 87.8 %reduce-scatter.3.cloned.1.call-done = f32[1,16,512]{2,1,0:T(8,128)} async-done(((f32[1,512,512]{2,1,0:T(8,128)}), f32[1,16,512]{2,1,0:T(8,128)}) %reduce-scatter.3.cloned.1.call-update) | async-done | bytes 32784 | tf_op jit(solution)/shard_map/reduce_scatter | solution.py:38
  329.5 1.4 multiply_reduce_fusion.5
  330.9 75.7 %psum.71 = f32[]{:T(128)} all-reduce(f32[]{:T(128)} %multiply_reduce_fusion.5), channel_id=1, replica_groups=mesh['term'=32,'sector'=8] {'term','sector'}, use_global_device_ids=true, to_apply=%region_4.6 | all-reduce | flops 1 | bytes 8 | tf_op jit(solution)/shard_map/psum | solution.py:42
  407.3 1.5 multiply_reduce_fusion.4
  408.8 73.4 %psum.72 = f32[]{:T(128)} all-reduce(f32[]{:T(128)} %get-tuple-element.16), channel_id=1, replica_groups=mesh['term'=32,'sector'=8] {'term','sector'}, use_global_device_ids=true, to_apply=%region_6.8 | all-reduce | flops 1 | bytes 8 | tf_op jit(solution)/shard_map/psum | solution.py:44
  483.5 73.4 %psum.73 = f32[]{:T(128)} all-reduce(f32[]{:T(128)} %multiply_reduce_fusion.3), channel_id=1, replica_groups=mesh['term'=32,'sector'=8] {'term','sector'}, use_global_device_ids=true, to_apply=%region_8.10 | all-reduce | flops 1 | bytes 8 | tf_op jit(solution)/shard_map/psum | solution.py:46
  557.7 46.8 %all_gather.14 = bf16[1,512,512]{2,1,0:T(8,128)(2,1)} all-gather(bf16[1,16,512]{2,1,0:T(8,128)(2,1)S(1)} %get-tuple-element.14), channel_id=1, replica_groups=mesh['term'=32,'sector'=8] {'term'}, dimensions={1}, use_global_device_ids=true | all-gather | bytes 540672 | tf_op jit(solution)/shard_map/all_gather | solution.py:28
  604.7 87.0 %all-gather.5.cloned.1.call-done = bf16[8,512,512]{2,1,0:T(8,128)(2,1)} async-done(((bf16[1,512,512]{2,1,0:T(8,128)(2,1)}), bf16[8,512,512]{2,1,0:T(8,128)(2,1)}) %all-gather.5.cloned.1.call-update) | async-done | bytes 4194320 | tf_op jit(solution)/shard_map/all_gather | solution.py:29
  691.7 5.0 gather_fusion.1
  696.7 10.3 %fusion.23 = f32[1,512,512]{2,1,0:T(8,128)} fusion(bf16[8,1,512,512]{3,2,1,0:T(8,128)(2,1)} %param.10, bf16[8,512,512]{2,1,0:T(8,128)(2,1)} %gather_fusion.1, bf16[8,1,512,512]{3,2,1,0:T(8,128)(2,1)} %param.9, pred[8]{0:T(512)(128)(4,1)S(1)} %and_reduce_fusion), kind=kOutput, calls=%fused_computation.23 | convolution fusion | flops 4299161600 | bytes 13631496 | tf_op jit(solution)/shard_map/tpij,tpkj->pik/dot_general | solution.py:35
  707.0 87.9 %reduce-scatter.5.cloned.1.call-done = f32[1,16,512]{2,1,0:T(8,128)} async-done(((f32[1,512,512]{2,1,0:T(8,128)}), f32[1,16,512]{2,1,0:T(8,128)}) %reduce-scatter.5.cloned.1.call-update) | async-done | bytes 32784 | tf_op jit(solution)/shard_map/reduce_scatter | solution.py:38
  794.8 2.1 multiply_reduce_fusion.2
  796.9 15.8 %all-reduce.1 = (f32[]{:T(128)}, f32[]{:T(128)}, f32[]{:T(128)}) all-reduce(f32[]{:T(128)} %get-tuple-element.5, f32[]{:T(128)} %get-tuple-element.6, f32[]{:T(128)} %get-tuple-element.4), channel_id=1, replica_groups=mesh['term'=32,'sector'=8] {'sector'}, use_global_device_ids=true, to_apply=%region_17.19 | all-reduce | flops 3 | bytes 24 | tf_op jit(solution)/shard_map/psum | solution.py:50
  812.7 76.3 %all-reduce = (f32[]{:T(128)}, f32[]{:T(128)}, f32[]{:T(128)}) all-reduce(f32[]{:T(128)} %get-tuple-element.10, f32[]{:T(128)} %get-tuple-element.11, f32[]{:T(128)} %get-tuple-element.12), channel_id=1, replica_groups=mesh['term'=32,'sector'=8] {'term'}, use_global_device_ids=true, to_apply=%region_18.20 | all-reduce | flops 3 | bytes 24 | tf_op jit(solution)/shard_map/psum | solution.py:49
  (23 shorter events, 3.2 us)
Async XLA Ops:
  7.2 219.2 %all-gather.3.cloned.1.call-start = ((), (), s32[]{:S(2)}) async-start(), calls=%async_computation.2 | async-start | bytes 4718592 | tf_op jit(solution)/shard_map/all_gather | solution.py:29
  138.2 191.2 %reduce-scatter.3.cloned.1.call-start = ((), (), s32[]{:S(2)}) async-start(), calls=%async_computation.3 | async-start | bytes 1081344 | tf_op jit(solution)/shard_map/reduce_scatter | solution.py:38
  231.3 98.2 %copy-start = (f32[1,16,512]{2,1,0:T(8,128)S(1)}, f32[1,16,512]{2,1,0:T(8,128)}, u32[]{:S(2)}) copy-start(f32[1,16,512]{2,1,0:T(8,128)} %param.8) | copy-start | bytes 98308
  231.3 176.0 %copy-start.3 = (f32[1,16,512]{2,1,0:T(8,128)S(1)}, f32[1,16,512]{2,1,0:T(8,128)}, u32[]{:S(2)}) copy-start(f32[1,16,512]{2,1,0:T(8,128)} %param.11) | copy-start | bytes 98308
  241.6 450.1 %all-gather.5.cloned.1.call-start = ((), (), s32[]{:S(2)}) async-start(), calls=%async_computation.4 | async-start | bytes 4718592 | tf_op jit(solution)/shard_map/all_gather | solution.py:29
  557.6 237.2 %copy-start.2 = (f32[1,16,512]{2,1,0:T(8,128)}, f32[1,16,512]{2,1,0:T(8,128)S(1)}, u32[]{:S(2)}) copy-start(f32[1,16,512]{2,1,0:T(8,128)S(1)} %get-tuple-element.15) | copy-start | bytes 98308
  604.4 190.4 %reduce-scatter.5.cloned.1.call-start = ((), (), s32[]{:S(2)}) async-start(), calls=%async_computation.5 | async-start | bytes 1081344 | tf_op jit(solution)/shard_map/reduce_scatter | solution.py:38
  696.7 98.2 %copy-start.1 = (f32[1,16,512]{2,1,0:T(8,128)S(1)}, f32[1,16,512]{2,1,0:T(8,128)}, u32[]{:S(2)}) copy-start(f32[1,16,512]{2,1,0:T(8,128)} %reduce-scatter.3.cloned.1.call-done) | copy-start | bytes 98308
Sparse Core Ops, SparseCore 0:
  138.4 87.9 all-gather.2
  241.7 87.6 reduce-scatter.2
  604.6 87.0 all-gather.4
  707.1 87.6 reduce-scatter.4
